TPU v7x, 128 devices: a whole 4x4x4 slice. The times are simulated.
128 devices in a mesh: frame: 32 (over y, x, core), tile: 4 (over z).
Axes of the slice: x: 4, y: 4, z: 4, core: 2. Of those that a mesh axis runs over, the one named last changes fastest.
Arguments:
- counts: float32 [1024, 524288], P('frame', 'tile'), may hold values from -1 to 23
- dark_level: float32 [524288], P('tile'), may hold values from 0 to 2
- flat_field: float32 [524288], P('tile'), may hold values from 0.5 to 2
- valid_pixel: int32 [524288], P('tile'), may hold values 0 or 1
- cycle_label: int32 [524288], P('tile'), may hold values from 0 to 32, as said below
- cycle_order: int32 [4, 32, 32], P('tile'), may hold values from 0 to 1024, as said below
- age_bin: int32 [1024], replicated, may hold values from 0 to 15, never falling along the last dimension, each value on 1 to 128 neighbouring positions
Outputs:
- two_time: float32 [32, 1024, 1024], P('frame', 'tile')
- aged_correlation: float32 [32, 16, 1024], P('frame', None, 'tile')
- mean_image: float32 [4, 32, 4096], P('tile', 'frame')
Inputs may be any that keep to these rules, and one draw needn't show every extreme that they name: cycle_order[t, q, :] lists distinct pixel blocks of module t (indices within the module) whose nominal cycle is q, then 131072 // 128 in the unused entries; no block is listed twice in a module; some cycle fills all entries of each module. `cycle_label`: most pixels carry the nominal cycle of the block under which cycle_order lists them.
All inputs are finite; a program needn't handle non-finite values. No bound on the sum of `valid_pixel` on one device may be relied on, other than what follows from the above.
Results may differ from a plain program's by a relative error of at most 0.0003.
Values may be sent and summed in bfloat16 or wider, within the bound.
A program may use at most 128 MiB of HBM per device.

v0:
```python
import jax
import jax.numpy as jnp
from jax import lax
from jax.sharding import PartitionSpec as P

BLK = 128
NA = 16


def band_rows(cmap_rows, age_bin):
    cycle_count, row_count, col_width = cmap_rows.shape
    padded_map = jnp.concatenate([cmap_rows, jnp.zeros_like(cmap_rows)], axis=2)
    span = col_width + row_count
    flattened = jnp.concatenate(
        [
            padded_map.reshape(cycle_count, row_count * span),
            jnp.zeros((cycle_count, row_count), jnp.float32),
        ],
        axis=1,
    )
    skewed_map = flattened.reshape(cycle_count, row_count, span + 1)[:, :, :col_width]
    onehot = (age_bin[None, :] == jnp.arange(NA, dtype=jnp.int32)[:, None]).astype(jnp.float32)
    return jnp.einsum("bi,rid->rbd", onehot, skewed_map, precision=lax.Precision.HIGHEST)


def lag_counts(age_bin, lag_start, lag_count):
    frames = age_bin.shape[0]
    lag_values = lag_start + jnp.arange(lag_count, dtype=jnp.int32)
    inside = (jnp.arange(frames, dtype=jnp.int32)[:, None] + lag_values[None, :] < frames).astype(
        jnp.float32
    )
    onehot = (age_bin[None, :] == jnp.arange(NA, dtype=jnp.int32)[:, None]).astype(jnp.float32)
    return jnp.dot(onehot, inside, precision=lax.Precision.HIGHEST)


def gram_block(frame_block, exchanged):
    return jnp.einsum("irp,jrp->irj", frame_block, exchanged, preferred_element_type=jnp.float32)


def block_rows(values, block_ids, block_total):
    return jnp.take(values.reshape(block_total, BLK), block_ids, axis=0)


def local(counts, dark_level, flat_field, valid_pixel, cycle_label, cycle_order, age_bin):
    pix_module = dark_level.shape[0]
    block_total = pix_module // BLK
    block_order = cycle_order[0]
    cycle_total, block_count = block_order.shape
    slot = block_count * BLK
    frame_part = counts.shape[0]
    is_padding = (block_order >= block_total)[:, :, None]
    block_ids = jnp.where(block_order >= block_total, 0, block_order).reshape(-1)
    cycle_ids = jnp.arange(cycle_total, dtype=jnp.int32)[:, None, None]
    usable = (
        block_rows(valid_pixel, block_ids, block_total)
        .reshape(cycle_total, block_count, BLK)
        .astype(jnp.float32)
    )
    matching = (
        block_rows(cycle_label, block_ids, block_total).reshape(cycle_total, block_count, BLK)
        == cycle_ids
    ).astype(jnp.float32)
    member_blocks = jnp.where(is_padding, 0.0, usable * matching)
    member = member_blocks.reshape(cycle_total, slot)
    slot_gain = block_rows(flat_field, block_ids, block_total) * member_blocks.reshape(
        cycle_total * block_count, BLK
    )
    slot_dark = block_rows(dark_level, block_ids, block_total)
    columns = jnp.take(counts.reshape(frame_part, block_total, BLK), block_ids, axis=1)
    sorted_frames = (
        ((columns - slot_dark[None]) * slot_gain[None])
        .astype(jnp.bfloat16)
        .reshape(frame_part, cycle_total, slot)
    )
    exchanged = lax.all_to_all(sorted_frames, "frame", split_axis=1, concat_axis=0, tiled=True)
    frames = exchanged.shape[0]
    cycle_count = exchanged.shape[1]
    first_cycle = lax.axis_index("frame") * cycle_count
    own_member = lax.dynamic_slice_in_dim(member, first_cycle, cycle_count, 0)
    widened = exchanged.astype(jnp.float32)
    cycle_sums = jnp.transpose(jnp.sum(widened, axis=2), (1, 0))
    image = jnp.sum(widened, axis=0) / frames
    totals, pixel_sums = lax.psum((cycle_sums, jnp.sum(own_member, axis=1)), "tile")
    pixel_total = jnp.maximum(pixel_sums, 1.0)
    clamped = jnp.maximum(totals / pixel_total[:, None], 1.0)
    row_count = frames // lax.axis_size("tile")
    row_start = lax.axis_index("tile") * row_count
    gram_part = lax.psum_scatter(
        gram_block(exchanged, exchanged), "tile", scatter_dimension=0, tiled=True
    )
    row_clamped = lax.dynamic_slice_in_dim(clamped, row_start, row_count, 1)
    two_time = jnp.transpose(gram_part, (1, 0, 2)) / (
        pixel_total[:, None, None] * row_clamped[:, :, None] * clamped[:, None, :]
    )
    lag_total = jnp.maximum(lag_counts(age_bin, row_start, row_count), 1.0)
    whole_map = lax.all_gather(two_time, "tile", axis=1, tiled=True)
    band_sum = lax.dynamic_slice_in_dim(band_rows(whole_map, age_bin), row_start, row_count, 2)
    return (two_time, band_sum / lag_total[None], image[None])


def solution(mesh):
    in_specs = (
        P("frame", "tile"),
        P("tile"),
        P("tile"),
        P("tile"),
        P("tile"),
        P("tile", None, None),
        P(),
    )
    out_specs = (P("frame", "tile", None), P("frame", None, "tile"), P("tile", "frame", None))
    return jax.shard_map(local, mesh=mesh, in_specs=in_specs, out_specs=out_specs, check_vma=False)
```

profile of v0, /device:TPU:1, one launch (start us, length us, event | category | flops | bytes accessed | tf_op | source)
XLA Modules:
  0.0 456.4 jit_solution(15316091511293030886)
XLA Ops:
  7.2 0.0 copy-start
  7.2 0.0 reduce-scatter.2.cloned.1.call-start
  7.2 0.8 squeeze.8
  8.1 0.8 squeeze.9
  8.9 0.7 bitcast_compare_fusion
  9.6 11.8 %copy_bitcast_fusion = f32[32,1024,128]{2,0,1:T(8,128)} fusion(f32[32,131072]{1,0:T(8,128)} %param.11), kind=kLoop, calls=%fused_computation.7 | loop fusion | bytes 33554432 | tf_op jit(solution)/shard_map/reshape | solution.py:69
  21.4 18.1 %gather_fusion = f32[1024,32,128]{2,1,0:T(8,128)} fusion(f32[32,1024,128]{2,0,1:T(8,128)} %copy_bitcast_fusion, s32[1024]{0:T(1024)S(1)} %broadcast_clamp_fusion), kind=kCustom, calls=%fused_computation.4 | custom fusion | bytes 33558528 | tf_op jit(solution)/shard_map/jit(_take)/gather | solution.py:69
  39.6 14.1 %copy.25 = f32[32,1024,128]{2,1,0:T(8,128)} copy(f32[32,1024,128]{2,0,1:T(8,128)} %bitcast.63) | data formatting | bytes 33554432 | tf_op jit(solution)/shard_map/jit(_take)/gather | solution.py:69
  53.7 0.0 copy-start.3
  53.7 18.3 %gather.13 = f32[32,32,4096]{2,1,0:T(8,128)} reshape(f32[32,1024,128]{2,1,0:T(8,128)} %copy.25) | data formatting | bytes 33554432 | tf_op jit(solution)/shard_map/jit(_take)/gather | solution.py:69
  72.0 0.0 copy-done
  72.0 0.0 copy-start.4
  72.0 0.0 copy-start.5
  72.0 2.8 gather_fusion.1
  74.8 0.0 copy-done.3
  74.8 2.8 gather_fusion.4
  77.6 0.1 eq.39
  77.7 0.0 copy-done.4
  77.7 2.8 gather_fusion.3
  80.5 0.0 copy-done.5
  80.5 2.8 gather_fusion.2
  83.3 0.9 broadcast_select_fusion.1
  84.3 0.1 mul.65
  84.4 0.1 sub.11
  84.5 0.2 broadcast_in_dim.79
  84.7 0.1 copy.41
  84.8 9.5 %multiply_convert_fusion = bf16[32,32,4096]{2,1,0:T(8,128)(2,1)} fusion(f32[32,32,4096]{2,1,0:T(8,128)} %gather.13, f32[32,4096]{1,0:T(8,128)S(1)} %mul.65, f32[32,4096]{1,0:T(8,128)S(1)} %sub.11, pred[32,4096]{1,0:T(8,128)(4,1)S(1)} %bitcast.69), kind=kLoop, calls=%fused_computation.8 | loop fusion | flops 16777216 | bytes 26345472 | tf_op jit(solution)/shard_map/convert_element_type | solution.py:72
  94.2 11.2 %copy.26 = bf16[32,32,4096]{2,0,1:T(8,128)(2,1)} copy(bf16[32,32,4096]{2,1,0:T(8,128)(2,1)} %multiply_convert_fusion) | data formatting | bytes 16777216 | tf_op jit(solution)/shard_map/convert_element_type | solution.py:72
  105.4 104.3 %all_to_all.15 = bf16[32,32,4096]{2,0,1:T(8,128)(2,1)S(1)} all-to-all(bf16[32,32,4096]{2,0,1:T(8,128)(2,1)} %copy.26), channel_id=1, replica_groups=mesh['frame'=32,'tile'=4] {'frame'}, dimensions={1} | all-to-all | bytes 16777216 | tf_op jit(solution)/shard_map/all_to_all | solution.py:75
  209.7 0.0 copy-start.2
  209.7 3.2 copy-done.2
  212.9 10.4 %convolution_bitcast_fusion = f32[1024,1,1024]{0,2,1:T(8,128)} fusion(bf16[1024,4096]{1,0:T(8,128)(2,1)S(1)} %bitcast.65), kind=kOutput, calls=%fused_computation.13 | convolution fusion | flops 8589934592 | bytes 12582912 | tf_op jit(solution)/shard_map/irp,jrp->irj/dot_general | solution.py:37
  223.3 0.0 reduce-scatter.2.cloned.1.call-update
  223.3 0.0 all-gather.2.cloned.1.call-start
  223.4 0.2 broadcast_select_fusion
  223.6 0.1 convert_element_type.25
  223.7 0.1 reshape.229
  223.8 0.2 broadcast_in_dim.87
  224.0 0.1 copy.40
  224.1 0.7 fusion.7
  224.8 7.8 %convert_reduce_fusion = (f32[4096]{0:T(1024)S(1)}, f32[32,32]{1,0:T(8,128)S(1)}) fusion(bf16[32,32,4096]{2,0,1:T(8,128)(2,1)} %copy-done.2), kind=kLoop, calls=%fused_computation.5 | loop fusion | flops 12577792 | bytes 8409088 | tf_op jit(solution)/shard_map/reduce_sum | solution.py:82
  232.6 0.1 transpose.25
  232.7 12.1 %all-reduce.2 = (f32[1,1024]{1,0:T(1,128)S(1)}, f32[1]{0:T(128)}) all-reduce(f32[1,1024]{1,0:T(1,128)S(1)} %transpose.25, f32[1]{0:T(128)} %bitcast.13), channel_id=1, replica_groups=mesh['frame'=32,'tile'=4] {'tile'}, use_global_device_ids=true, to_apply=%region_4.7 | all-reduce | flops 1025 | bytes 8200 | tf_op jit(solution)/shard_map/psum | solution.py:83
  245.5 23.8 %reduce-scatter.2.cloned.1.call-done = f32[256,1,1024]{0,2,1:T(8,128)} async-done(((f32[1024,1,1024]{0,2,1:T(8,128)}), f32[256,1,1024]{0,2,1:T(8,128)}) %reduce-scatter.2.cloned.1.call-update) | async-done | bytes 1048592 | tf_op jit(solution)/shard_map/reduce_scatter | solution.py:88
  269.3 2.4 bitcast_divide_fusion
  271.7 0.0 all-gather.2.cloned.1.call-update
  271.7 0.6 broadcast_multiply_fusion
  272.3 2.5 copy.30
  274.9 44.7 %all-gather.2.cloned.1.call-done = f32[1,1024,1024]{1,2,0:T(8,128)} async-done(((f32[1,256,1024]{1,2,0:T(8,128)}), f32[1,1024,1024]{1,2,0:T(8,128)}) %all-gather.2.cloned.1.call-update) | async-done | bytes 4194320 | tf_op jit(solution)/shard_map/all_gather | solution.py:96
  319.6 5.4 %copy.32 = f32[1,1024,1024]{2,1,0:T(8,128)} copy(f32[1,1024,1024]{1,2,0:T(8,128)} %all-gather.2.cloned.1.call-done) | data formatting | bytes 8388608
  325.0 3.3 pad_bitcast_fusion
  328.2 12.5 %copy.36 = f32[1,1,1024,2048]{3,1,2,0:T(1,128)} copy(f32[1,1,1024,2048]{3,2,1,0:T(8,128)S(1)} %pad_bitcast_fusion) | data formatting | bytes 16777216
  340.8 0.0 copy-start.1
  340.8 91.3 %pad_reduce_fusion = f32[2098176]{0:T(1024)} fusion(f32[1,2097152]{1,0:T(1,128)} %bitcast.64), kind=kLoop, calls=%fused_computation.9 | loop fusion | bytes 16781312 | tf_op jit(solution)/shard_map/concatenate | solution.py:14
  432.1 0.0 copy-start.6
  432.1 12.9 %reshape.231 = f32[1,1024,2049]{2,1,0:T(8,128)} reshape(f32[2098176]{0:T(1024)} %pad_reduce_fusion) | data formatting | bytes 16785408 | tf_op jit(solution)/shard_map/reshape | solution.py:21
  445.0 0.0 copy-done.6
  445.0 3.6 fusion
  448.6 0.9 fusion.2
  449.6 0.0 copy-done.1
  (8 shorter events, 0.1 us)
Async XLA Ops:
  7.2 64.8 %copy-start = (f32[131072]{0:T(1024)S(1)}, f32[131072]{0:T(1024)}, u32[]{:S(2)}) copy-start(f32[131072]{0:T(1024)} %param.12) | copy-start | bytes 1572868
  7.2 262.1 %reduce-scatter.2.cloned.1.call-start = ((), (), s32[]{:S(2)}) async-start(), calls=%async_computation.2 | async-start | bytes 5242880 | tf_op jit(solution)/shard_map/reduce_scatter | solution.py:88
  53.7 21.1 %copy-start.3 = (s32[131072]{0:T(1024)S(1)}, s32[131072]{0:T(1024)}, u32[]{:S(2)}) copy-start(s32[131072]{0:T(1024)} %param.14) | copy-start | bytes 1572868
  72.0 5.7 %copy-start.4 = (s32[131072]{0:T(1024)S(1)}, s32[131072]{0:T(1024)}, u32[]{:S(2)}) copy-start(s32[131072]{0:T(1024)} %param.15) | copy-start | bytes 1572868
  72.0 8.6 %copy-start.5 = (f32[131072]{0:T(1024)S(1)}, f32[131072]{0:T(1024)}, u32[]{:S(2)}) copy-start(f32[131072]{0:T(1024)} %param.13) | copy-start | bytes 1572868
  209.7 3.2 copy-start.2
  223.3 96.3 %all-gather.2.cloned.1.call-start = ((), (), s32[]{:S(2)}) async-start(), calls=%async_computation.3 | async-start | bytes 5242880 | tf_op jit(solution)/shard_map/all_gather | solution.py:96
  340.8 108.8 %copy-start.1 = (f32[131072]{0:T(1024)S(1)}, f32[131072]{0:T(1024)}, u32[]{:S(2)}) copy-start(f32[131072]{0:T(1024)} %param.12) | copy-start | bytes 1572868
  432.1 12.9 %copy-start.6 = (s32[1024]{0:T(1024)S(1)}, s32[1024]{0:T(1024)}, u32[]{:S(2)}) copy-start(s32[1024]{0:T(1024)} %param.17) | copy-start | bytes 12292
Sparse Core Ops, SparseCore 0:
  223.4 45.8 reduce-scatter.1
  271.9 47.7 all-gather.1
where the time goes:
time: 458 us; the launch traced here: 456 us
  local copies, waits for them, and re-layouts  219 us (48%)
  blocking collectives  116 us (25%)
  waiting for transfers between devices  68.6 us (15%)
  other arithmetic  22.9 us (5%)
  matrix products  15 us (3%)
  between operations  14.9 us (3%)
    all_to_all x1, blocking collectives, local(): lax.all_to_all(sorted_frames, 'frame', split_axis=1, concat_axis=0, tiled...  104 us
    concatenate x1, local copies, waits for them, and re-layouts, band_rows(): jnp.concatenate([padded_map.reshape(cycle_count, row_count * span), jnp.z...  91.3 us
    gather x3, local copies, waits for them, and re-layouts, local(): jnp.take(counts.reshape(frame_part, block_total, BLK), block_ids, axis=1)  50.5 us
    all_gather x1, waiting for transfers between devices, local(): whole_map = lax.all_gather(two_time, 'tile', axis=1, tiled=True)  44.7 us
    unnamed x20, local copies, waits for them, and re-layouts  27.1 us
    reduce_scatter x1, waiting for transfers between devices, local(): lax.psum_scatter(gram_block(exchanged, exchanged), 'tile', scatter_dimens...  23.8 us
    reshape x1, local copies, waits for them, and re-layouts, band_rows(): flattened.reshape(cycle_count, row_count, span + 1)[:, :, :col_width]  12.9 us
    psum x1, blocking collectives, local(): lax.psum((cycle_sums, jnp.sum(own_member, axis=1)), 'tile')  12.1 us
  transfers between devices with their start and end apart: 2, of which 2 were waited for; matrix products, arithmetic and copies ran while one was open for 3% of the time, Pallas kernels for 0%

commit v1 on v0

--- a/solution.py
+++ b/solution.py
@@ -93,7 +93,8 @@
         pixel_total[:, None, None] * row_clamped[:, :, None] * clamped[:, None, :]
     )
     lag_total = jnp.maximum(lag_counts(age_bin, row_start, row_count), 1.0)
-    whole_map = lax.all_gather(two_time, "tile", axis=1, tiled=True)
+    repeated = jnp.stack([two_time] * lax.axis_size("tile"))
+    whole_map = jnp.concatenate(lax.all_to_all(repeated, "tile", 0, 0), axis=1)
     band_sum = lax.dynamic_slice_in_dim(band_rows(whole_map, age_bin), row_start, row_count, 2)
     return (two_time, band_sum / lag_total[None], image[None])
 

time: 458 us -> 460 us (level)
  starting transfers between devices: 0.08 us -> 5.1 us
    all_to_all x0 -> x1, waiting for transfers between devices: none -> 45.9 us  [local(): whole_map = jnp.concatenate(lax.all_to_all(repeated, 'tile', 0, 0), axis=1)]
    all_gather x1 -> x0, waiting for transfers between devices: 44.7 us -> none  [local(): whole_map = lax.all_gather(two_time, 'tile', axis=1, tiled=True)]
    unnamed x20 -> x21, local copies, waits for them, and re-layouts: 27.1 us -> 20.5 us
    all_to_all x0 -> x1, starting transfers between devices: none -> 5.06 us  [local(): whole_map = jnp.concatenate(lax.all_to_all(repeated, 'tile', 0, 0), axis=1)]
  transfers between devices with their start and end apart: 2 -> 2, of which waited for: 2 -> 2; matrix products, arithmetic and copies ran while one was open for 3% -> 2% of each run, Pallas kernels for 0% -> 0%
where the time goes in v1:
time: 460 us; the launch traced here: 458 us
  local copies, waits for them, and re-layouts  215 us (47%)
  blocking collectives  116 us (25%)
  waiting for transfers between devices  70 us (15%)
  other arithmetic  22.1 us (5%)
  matrix products  15 us (3%)
  between operations  14.9 us (3%)
  starting transfers between devices  5.1 us (1%)
    all_to_all x1, blocking collectives, local(): lax.all_to_all(sorted_frames, 'frame', split_axis=1, concat_axis=0, tiled...  104 us
    concatenate x1, local copies, waits for them, and re-layouts, band_rows(): jnp.concatenate([padded_map.reshape(cycle_count, row_count * span), jnp.z...  91.3 us
    gather x3, local copies, waits for them, and re-layouts, local(): jnp.take(counts.reshape(frame_part, block_total, BLK), block_ids, axis=1)  50.5 us
    all_to_all x1, waiting for transfers between devices, local(): whole_map = jnp.concatenate(lax.all_to_all(repeated, 'tile', 0, 0), axis=1)  45.9 us
    reduce_scatter x1, waiting for transfers between devices, local(): lax.psum_scatter(gram_block(exchanged, exchanged), 'tile', scatter_dimens...  24.1 us
    unnamed x21, local copies, waits for them, and re-layouts  20.5 us
    reshape x1, local copies, waits for them, and re-layouts, band_rows(): flattened.reshape(cycle_count, row_count, span + 1)[:, :, :col_width]  12.9 us
    psum x1, blocking collectives, local(): lax.psum((cycle_sums, jnp.sum(own_member, axis=1)), 'tile')  11.9 us
  transfers between devices with their start and end apart: 2, of which 2 were waited for; matrix products, arithmetic and copies ran while one was open for 2% of the time, Pallas kernels for 0%

profile of v1, /device:TPU:1, one launch (start us, length us, event | category | flops | bytes accessed | tf_op | source)
XLA Modules:
  0.0 458.1 jit_solution(3572855804712538275)
XLA Ops:
  7.2 0.0 copy-start
  7.2 0.0 reduce-scatter.2.cloned.1.call-start
  7.2 0.8 squeeze.8
  8.1 0.8 squeeze.9
  8.9 0.7 bitcast_compare_fusion
  9.6 11.8 %copy_bitcast_fusion = f32[32,1024,128]{2,0,1:T(8,128)} fusion(f32[32,131072]{1,0:T(8,128)} %param.11), kind=kLoop, calls=%fused_computation.7 | loop fusion | bytes 33554432 | tf_op jit(solution)/shard_map/reshape | solution.py:69
  21.4 18.1 %gather_fusion = f32[1024,32,128]{2,1,0:T(8,128)} fusion(f32[32,1024,128]{2,0,1:T(8,128)} %copy_bitcast_fusion, s32[1024]{0:T(1024)S(1)} %broadcast_clamp_fusion), kind=kCustom, calls=%fused_computation.4 | custom fusion | bytes 33558528 | tf_op jit(solution)/shard_map/jit(_take)/gather | solution.py:69
  39.6 14.1 %copy.26 = f32[32,1024,128]{2,1,0:T(8,128)} copy(f32[32,1024,128]{2,0,1:T(8,128)} %bitcast.66) | data formatting | bytes 33554432 | tf_op jit(solution)/shard_map/jit(_take)/gather | solution.py:69
  53.7 0.0 copy-start.3
  53.7 18.3 %gather.13 = f32[32,32,4096]{2,1,0:T(8,128)} reshape(f32[32,1024,128]{2,1,0:T(8,128)} %copy.26) | data formatting | bytes 33554432 | tf_op jit(solution)/shard_map/jit(_take)/gather | solution.py:69
  72.0 0.0 copy-done
  72.0 0.0 copy-start.4
  72.0 0.0 copy-start.5
  72.0 2.8 gather_fusion.1
  74.8 0.0 copy-done.3
  74.8 2.8 gather_fusion.4
  77.6 0.1 eq.39
  77.7 0.0 copy-done.4
  77.7 2.8 gather_fusion.3
  80.5 0.0 copy-done.5
  80.5 2.8 gather_fusion.2
  83.3 0.9 broadcast_select_fusion.1
  84.3 0.1 mul.74
  84.4 0.1 sub.11
  84.5 0.2 broadcast_in_dim.79
  84.7 0.1 copy.41
  84.8 9.5 %multiply_convert_fusion = bf16[32,32,4096]{2,1,0:T(8,128)(2,1)} fusion(f32[32,32,4096]{2,1,0:T(8,128)} %gather.13, f32[32,4096]{1,0:T(8,128)S(1)} %mul.74, f32[32,4096]{1,0:T(8,128)S(1)} %sub.11, pred[32,4096]{1,0:T(8,128)(4,1)S(1)} %bitcast.72), kind=kLoop, calls=%fused_computation.8 | loop fusion | flops 16777216 | bytes 26345472 | tf_op jit(solution)/shard_map/convert_element_type | solution.py:72
  94.2 11.2 %copy.27 = bf16[32,32,4096]{2,0,1:T(8,128)(2,1)} copy(bf16[32,32,4096]{2,1,0:T(8,128)(2,1)} %multiply_convert_fusion) | data formatting | bytes 16777216 | tf_op jit(solution)/shard_map/convert_element_type | solution.py:72
  105.4 104.3 %all_to_all.20 = bf16[32,32,4096]{2,0,1:T(8,128)(2,1)S(1)} all-to-all(bf16[32,32,4096]{2,0,1:T(8,128)(2,1)} %copy.27), channel_id=1, replica_groups=mesh['frame'=32,'tile'=4] {'frame'}, dimensions={1} | all-to-all | bytes 16777216 | tf_op jit(solution)/shard_map/all_to_all | solution.py:75
  209.7 0.0 copy-start.2
  209.7 3.2 copy-done.2
  212.9 10.4 %convolution_bitcast_fusion = f32[1024,1,1024]{0,2,1:T(8,128)} fusion(bf16[1024,4096]{1,0:T(8,128)(2,1)S(1)} %bitcast.68), kind=kOutput, calls=%fused_computation.13 | convolution fusion | flops 8589934592 | bytes 12582912 | tf_op jit(solution)/shard_map/irp,jrp->irj/dot_general | solution.py:37
  223.3 0.0 reduce-scatter.2.cloned.1.call-update
  223.3 0.2 broadcast_select_fusion
  223.5 0.1 convert_element_type.25
  223.6 0.1 reshape.257
  223.8 0.2 broadcast_in_dim.87
  224.0 0.1 copy.40
  224.0 0.7 fusion.7
  224.7 7.8 %convert_reduce_fusion = (f32[4096]{0:T(1024)S(1)}, f32[32,32]{1,0:T(8,128)S(1)}) fusion(bf16[32,32,4096]{2,0,1:T(8,128)(2,1)} %copy-done.2), kind=kLoop, calls=%fused_computation.5 | loop fusion | flops 12577792 | bytes 8409088 | tf_op jit(solution)/shard_map/reduce_sum | solution.py:82
  232.6 0.1 transpose.27
  232.6 11.9 %all-reduce.2 = (f32[1,1024]{1,0:T(1,128)S(1)}, f32[1]{0:T(128)}) all-reduce(f32[1,1024]{1,0:T(1,128)S(1)} %transpose.27, f32[1]{0:T(128)} %bitcast.13), channel_id=1, replica_groups=mesh['frame'=32,'tile'=4] {'tile'}, use_global_device_ids=true, to_apply=%region_4.7 | all-reduce | flops 1025 | bytes 8200 | tf_op jit(solution)/shard_map/psum | solution.py:83
  245.2 24.1 %reduce-scatter.2.cloned.1.call-done = f32[256,1,1024]{0,2,1:T(8,128)} async-done(((f32[1024,1,1024]{0,2,1:T(8,128)}), f32[256,1,1024]{0,2,1:T(8,128)}) %reduce-scatter.2.cloned.1.call-update) | async-done | bytes 1048592 | tf_op jit(solution)/shard_map/reduce_scatter | solution.py:88
  269.3 1.4 bitcast_divide_fusion
  270.7 0.3 copy.30
  271.1 0.0 copy-start.6
  271.1 2.5 stack.2
  273.6 5.1 %all-to-all-start.1 = ((f32[4,1,256,1024]{3,2,1,0:T(8,128)}), f32[4,1,256,1024]{3,2,1,0:T(8,128)}, u32[]{:S(2)}, u32[]{:S(2)}) async-start(f32[4,1,256,1024]{3,2,1,0:T(8,128)} %stack.2), calls=%async_computation.2 | async-start | bytes 8388608 | tf_op jit(solution)/shard_map/all_to_all | solution.py:97
  278.7 0.6 broadcast_multiply_fusion
  279.3 0.0 copy-done.6
  279.3 0.2 bitcast_divide_fusion.1
  279.5 1.3 copy.31
  280.8 45.9 %all-to-all-done.1 = f32[4,1,256,1024]{3,2,1,0:T(8,128)} async-done(((f32[4,1,256,1024]{3,2,1,0:T(8,128)}), f32[4,1,256,1024]{3,2,1,0:T(8,128)}, u32[]{:S(2)}, u32[]{:S(2)}) %all-to-all-start.1) | async-done | bytes 4194336 | tf_op jit(solution)/shard_map/all_to_all | solution.py:97
  326.7 3.3 pad_bitcast_fusion
  329.9 12.5 %copy.36 = f32[1,1,1024,2048]{3,1,2,0:T(1,128)} copy(f32[1,1,1024,2048]{3,2,1,0:T(8,128)S(1)} %pad_bitcast_fusion) | data formatting | bytes 16777216
  342.5 0.0 copy-start.1
  342.5 91.3 %pad_reduce_fusion = f32[2098176]{0:T(1024)} fusion(f32[1,2097152]{1,0:T(1,128)} %bitcast.67), kind=kLoop, calls=%fused_computation.9 | loop fusion | bytes 16781312 | tf_op jit(solution)/shard_map/concatenate | solution.py:14
  433.8 0.0 copy-start.7
  433.8 12.9 %reshape.260 = f32[1,1024,2049]{2,1,0:T(8,128)} reshape(f32[2098176]{0:T(1024)} %pad_reduce_fusion) | data formatting | bytes 16785408 | tf_op jit(solution)/shard_map/reshape | solution.py:21
  446.7 0.0 copy-done.7
  446.7 3.6 fusion
  450.3 0.9 fusion.2
  451.3 0.0 copy-done.1
  (8 shorter events, 0.1 us)
Async XLA Ops:
  7.2 64.8 %copy-start = (f32[131072]{0:T(1024)S(1)}, f32[131072]{0:T(1024)}, u32[]{:S(2)}) copy-start(f32[131072]{0:T(1024)} %param.12) | copy-start | bytes 1572868
  7.2 262.1 %reduce-scatter.2.cloned.1.call-start = ((), (), s32[]{:S(2)}) async-start(), calls=%async_computation.3 | async-start | bytes 5242880 | tf_op jit(solution)/shard_map/reduce_scatter | solution.py:88
  53.7 21.1 %copy-start.3 = (s32[131072]{0:T(1024)S(1)}, s32[131072]{0:T(1024)}, u32[]{:S(2)}) copy-start(s32[131072]{0:T(1024)} %param.14) | copy-start | bytes 1572868
  72.0 5.7 %copy-start.4 = (s32[131072]{0:T(1024)S(1)}, s32[131072]{0:T(1024)}, u32[]{:S(2)}) copy-start(s32[131072]{0:T(1024)} %param.15) | copy-start | bytes 1572868
  72.0 8.6 %copy-start.5 = (f32[131072]{0:T(1024)S(1)}, f32[131072]{0:T(1024)}, u32[]{:S(2)}) copy-start(f32[131072]{0:T(1024)} %param.13) | copy-start | bytes 1572868
  209.7 3.2 copy-start.2
  271.1 8.2 %copy-start.6 = (f32[256,1,1024]{0,2,1:T(8,128)S(1)}, f32[256,1,1024]{0,2,1:T(8,128)}, u32[]{:S(2)}) copy-start(f32[256,1,1024]{0,2,1:T(8,128)} %reduce-scatter.2.cloned.1.call-done) | copy-start | bytes 3145732
  273.6 53.1 %all-to-all-start.1 = ((f32[4,1,256,1024]{3,2,1,0:T(8,128)}), f32[4,1,256,1024]{3,2,1,0:T(8,128)}, u32[]{:S(2)}, u32[]{:S(2)}) async-start(f32[4,1,256,1024]{3,2,1,0:T(8,128)} %stack.2), calls=%async_computation.2 | async-start | bytes 8388608 | tf_op jit(solution)/shard_map/all_to_all | solution.py:97
  342.5 108.8 %copy-start.1 = (f32[131072]{0:T(1024)S(1)}, f32[131072]{0:T(1024)}, u32[]{:S(2)}) copy-start(f32[131072]{0:T(1024)} %param.12) | copy-start | bytes 1572868
  433.8 12.9 %copy-start.7 = (s32[1024]{0:T(1024)S(1)}, s32[1024]{0:T(1024)}, u32[]{:S(2)}) copy-start(s32[1024]{0:T(1024)} %param.17) | copy-start | bytes 12292
Sparse Core Ops, SparseCore 0:
  223.4 45.8 reduce-scatter.1
